TPU v7x, 256 devices: a whole 4x4x8 slice. The times are simulated.
256 devices in a mesh: clip: 8 (over x_hi, y), feat: 32 (over z, x_lo, core).
Axes of the slice: x: 4 (x_hi: 2, x_lo: 2; x = x_hi * 2 + x_lo), y: 4, z: 8, core: 2. Of those that a mesh axis runs over, the one named last changes fastest.
Arguments:
- embeds: float32 [8192, 1152], P('clip', 'feat'), may hold values from -6 to 6
- frequencies: float32 [1152, 20480], P('clip', 'feat'), may hold values from -0.5 to 0.5
- phases: float32 [20480], P('feat'), may hold values from -3.140625 to 3.140625
- weights: float32 [20480, 128], P('feat', 'clip'), may hold values from -6 to 6
- labels: int32 [8192, 128], P('clip'), may hold values 0 or 1
Outputs:
- trained: float32 [20480, 128], P('feat', 'clip')
- scores: float32 [8192, 128], P('clip', 'feat')
All inputs are finite; a program needn't handle non-finite values. No bound on the sum of `labels` on one device may be relied on, other than what follows from the above.
Results may differ from a plain program's by a relative error of at most 0.0055.
Values may be sent and summed in bfloat16 or wider, within the bound.
A program may use at most 64 MiB of HBM per device.

v0:
```python
import math
import jax
import jax.numpy as jnp
from jax import lax
from jax.sharding import PartitionSpec as P

STEPS = 2


def summed_logits(partial_value):
    return lax.psum(partial_value, "feat")


def per_device(embeds, frequencies, phases, weights, labels):
    freq_full = lax.all_gather(frequencies, "clip", axis=0, tiled=True)
    feat_count = frequencies.shape[1]
    total_features = feat_count * lax.axis_size("feat")
    out_width = weights.shape[1] * lax.axis_size("clip")
    share_width = out_width // lax.axis_size("feat")
    angles = jnp.dot(
        lax.all_gather(embeds, "feat", axis=1, tiled=True),
        freq_full,
        precision=lax.Precision.HIGHEST,
        preferred_element_type=jnp.float32,
    )
    feature_scale = math.sqrt(2.0 / total_features)
    phi = (feature_scale * jnp.cos(angles + phases[None, :])).astype(jnp.bfloat16)
    full_weights = lax.all_gather(weights, "clip", axis=1, tiled=True)
    own_weights = weights
    weight_half = full_weights.astype(jnp.bfloat16)
    targets = labels.astype(jnp.float32)
    feat_start = lax.axis_index("feat") * share_width
    for step in range(STEPS):
        partial_value = jnp.dot(phi, weight_half, preferred_element_type=jnp.float32)
        summed = summed_logits(partial_value)
        residual = (jax.nn.sigmoid(summed) - targets).astype(jnp.bfloat16)
        grad_part = lax.dot_general(
            phi, residual, (((0,), (0,)), ((), ())), preferred_element_type=jnp.float32
        )
        grad_own = lax.psum_scatter(grad_part, "clip", scatter_dimension=1, tiled=True)
        own_weights = own_weights - 0.25 * grad_own
        weight_half = lax.all_gather(own_weights.astype(jnp.bfloat16), "clip", axis=1, tiled=True)
    partial_value = jnp.dot(phi, weight_half, preferred_element_type=jnp.float32)
    summed = summed_logits(partial_value)
    scores = lax.dynamic_slice_in_dim(summed, feat_start, share_width, 1)
    return (own_weights, scores)


def solution(mesh):
    placed = (P("clip", "feat"), P("clip", "feat"), P("feat"), P("feat", "clip"), P("clip", None))
    return jax.shard_map(
        per_device,
        mesh=mesh,
        in_specs=placed,
        out_specs=(P("feat", "clip"), P("clip", "feat")),
        check_vma=False,
    )
```

profile of v0, /device:TPU:1, one launch (start us, length us, event | category | flops | bytes accessed | tf_op | source)
XLA Modules:
  0.0 1094.3 jit_solution(6680869996846778569)
XLA Ops:
  7.2 0.7 all-gather.6.cloned.1.call-update
  7.9 0.7 all-gather.4.cloned.1.call-update
  8.7 0.8 convert
  9.5 29.4 %all_gather.17 = bf16[640,128]{0,1:T(8,128)(2,1)S(1)} all-gather(bf16[640,16]{0,1:T(8,128)(2,1)S(1)} %convert), channel_id=1, replica_groups=mesh['clip'=8,'feat'=32] {'clip'}, dimensions={1}, use_global_device_ids=true | all-gather | bytes 184320 | tf_op jit(solution)/shard_map/all_gather | solution.py:28
  38.8 43.2 %all-gather.6.cloned.1.call-done = f32[32,36,1024]{2,1,0:T(8,128)} async-done(((f32[1,36,1024]{2,1,0:T(8,128)}), f32[32,36,1024]{2,1,0:T(8,128)}) %all-gather.6.cloned.1.call-update) | async-done | bytes 4718608 | tf_op jit(solution)/shard_map/all_gather | solution.py:21
  82.0 5.2 reshape.6
  87.3 61.4 %all-gather.4.cloned.1.call-done = f32[1152,640]{1,0:T(8,128)} async-done(((f32[144,640]{1,0:T(8,128)}), f32[1152,640]{1,0:T(8,128)}) %all-gather.4.cloned.1.call-update) | async-done | bytes 2949136 | tf_op jit(solution)/shard_map/all_gather | solution.py:15
  148.6 23.3 %multiply_convert_fusion = bf16[1024,640]{1,0:T(8,128)(2,1)S(1)} fusion(f32[1152,1024]{1,0:T(8,128)} %reshape.6, f32[1152,640]{1,0:T(8,128)} %all-gather.4.cloned.1.call-done, f32[640]{0:T(1024)S(1)} %copy-done.3), kind=kOutput, calls=%fused_computation | convolution fusion | flops 9061662720 | bytes 8980992 | tf_op jit(solution)/shard_map/dot_general | solution.py:20
  172.0 1.3 fusion.12
  173.4 226.3 %all-reduce.4.cloned.1.call-done = f32[1024,128]{1,0:T(8,128)} async-done(((f32[1024,128]{1,0:T(8,128)}), f32[1024,128]{1,0:T(8,128)}) %all-reduce.4.cloned.1.call-update) | async-done | bytes 524304 | tf_op jit(solution)/shard_map/psum | solution.py:11
  399.6 2.2 fusion
  401.9 0.0 all-reduce.6.cloned.1.call-start
  401.9 75.8 %reduce-scatter.3.cloned.1.call-done = f32[640,16]{0,1:T(8,128)} async-done(((f32[640,128]{0,1:T(8,128)}), f32[640,16]{0,1:T(8,128)}) %reduce-scatter.3.cloned.1.call-update) | async-done | bytes 40976 | tf_op jit(solution)/shard_map/reduce_scatter | solution.py:40
  477.7 0.8 fusion.6
  478.5 27.9 %all_gather.18 = bf16[640,128]{0,1:T(8,128)(2,1)S(1)} all-gather(bf16[640,16]{0,1:T(8,128)(2,1)S(1)} %fusion.6), channel_id=1, replica_groups=mesh['clip'=8,'feat'=32] {'clip'}, dimensions={1}, use_global_device_ids=true | all-gather | bytes 184320 | tf_op jit(solution)/shard_map/all_gather | solution.py:42
  506.4 1.3 fusion.10
  507.7 234.8 %all-reduce.6.cloned.1.call-done = f32[1024,128]{1,0:T(8,128)} async-done(((f32[1024,128]{1,0:T(8,128)}), f32[1024,128]{1,0:T(8,128)}) %all-reduce.6.cloned.1.call-update) | async-done | bytes 524304 | tf_op jit(solution)/shard_map/psum | solution.py:11
  742.5 2.2 fusion.1
  744.8 75.8 %reduce-scatter.5.cloned.1.call-done = f32[640,16]{0,1:T(8,128)} async-done(((f32[640,128]{0,1:T(8,128)}), f32[640,16]{0,1:T(8,128)}) %reduce-scatter.5.cloned.1.call-update) | async-done | bytes 40976 | tf_op jit(solution)/shard_map/reduce_scatter | solution.py:40
  820.6 1.4 fusion.9
  822.0 27.9 %all_gather.19 = bf16[640,128]{0,1:T(8,128)(2,1)S(1)} all-gather(bf16[640,16]{0,1:T(8,128)(2,1)S(1)} %get-tuple-element.2), channel_id=1, replica_groups=mesh['clip'=8,'feat'=32] {'clip'}, dimensions={1}, use_global_device_ids=true | all-gather | bytes 184320 | tf_op jit(solution)/shard_map/all_gather | solution.py:42
  849.9 1.3 fusion.11
  851.3 234.8 %all-reduce.8.cloned.1.call-done = f32[1024,128]{0,1:T(8,128)} async-done(((f32[1024,128]{0,1:T(8,128)}), f32[1024,128]{0,1:T(8,128)}) %all-reduce.8.cloned.1.call-update) | async-done | bytes 524304 | tf_op jit(solution)/shard_map/psum | solution.py:11
  1086.1 1.4 constant_dynamic-slice_fusion
  (19 shorter events, 0.3 us)
Async XLA Ops:
  7.2 74.9 %all-gather.6.cloned.1.call-start = ((), (), s32[]{:S(2)}) async-start(), calls=%async_computation.8 | async-start | bytes 5406720 | tf_op jit(solution)/shard_map/all_gather | solution.py:21
  7.9 140.7 %all-gather.4.cloned.1.call-start = ((), (), s32[]{:S(2)}) async-start(), calls=%async_computation.2 | async-start | bytes 3317760 | tf_op jit(solution)/shard_map/all_gather | solution.py:15
  8.6 391.0 %all-reduce.4.cloned.1.call-start = ((), (), s32[]{:S(2)}) async-start(), calls=%async_computation.3 | async-start | bytes 1048576 | tf_op jit(solution)/shard_map/psum | solution.py:11
  38.8 109.8 %copy-start.3 = (f32[640]{0:T(1024)S(1)}, f32[640]{0:T(1024)}, u32[]{:S(2)}) copy-start(f32[640]{0:T(1024)} %param.7) | copy-start | bytes 7684
  172.0 227.6 %copy-start.2 = (s32[1024,128]{1,0:T(8,128)S(1)}, s32[1024,128]{1,0:T(8,128)}, u32[]{:S(2)}) copy-start(s32[1024,128]{1,0:T(8,128)} %param.9) | copy-start | bytes 1572868
  173.3 304.4 %copy-start = (f32[640,16]{0,1:T(8,128)S(1)}, f32[640,16]{0,1:T(8,128)}, u32[]{:S(2)}) copy-start(f32[640,16]{0,1:T(8,128)} %param.8) | copy-start | bytes 122884
  173.3 304.4 %reduce-scatter.3.cloned.1.call-start = ((), (), s32[]{:S(2)}) async-start(), calls=%async_computation.4 | async-start | bytes 368640 | tf_op jit(solution)/shard_map/reduce_scatter | solution.py:40
  401.9 340.7 %all-reduce.6.cloned.1.call-start = ((), (), s32[]{:S(2)}) async-start(), calls=%async_computation.5 | async-start | bytes 1048576 | tf_op jit(solution)/shard_map/psum | solution.py:11
  507.7 313.0 %copy-start.1 = (f32[640,16]{0,1:T(8,128)S(1)}, f32[640,16]{0,1:T(8,128)}, u32[]{:S(2)}) copy-start(f32[640,16]{0,1:T(8,128)} %reduce-scatter.3.cloned.1.call-done) | copy-start | bytes 122884
  507.7 312.9 %reduce-scatter.5.cloned.1.call-start = ((), (), s32[]{:S(2)}) async-start(), calls=%async_computation.6 | async-start | bytes 368640 | tf_op jit(solution)/shard_map/reduce_scatter | solution.py:40
  744.8 341.3 %all-reduce.8.cloned.1.call-start = ((), (), s32[]{:S(2)}) async-start(), calls=%async_computation.7 | async-start | bytes 1048576 | tf_op jit(solution)/shard_map/psum | solution.py:11
Sparse Core Ops, SparseCore 0:
  9.8 72.1 all-gather.5
  84.6 63.9 all-gather.3
  173.4 226.1 all-reduce.3
  403.3 74.3 reduce-scatter.2
  507.8 234.6 all-reduce.5
  746.2 74.3 reduce-scatter.4
  851.4 234.6 all-reduce.7
where the time goes:
time: 1090 us
  waiting for transfers between devices  954 us (88%)
  blocking collectives  85.1 us (8%)
  matrix products  31.7 us (3%)
  between operations  14.2 us (1%)
    psum x3, waiting for transfers between devices, summed_logits(): return lax.psum(partial_value, 'feat')  696 us
    reduce_scatter x2, waiting for transfers between devices, per_device(): lax.psum_scatter(grad_part, 'clip', scatter_dimension=1, tiled=True)  152 us
    all_gather x1, waiting for transfers between devices, per_device(): freq_full = lax.all_gather(frequencies, 'clip', axis=0, tiled=True)  61.4 us
    all_gather x2, blocking collectives, per_device(): lax.all_gather(own_weights.astype(jnp.bfloat16), 'clip', axis=1, tiled=True)  55.7 us
    all_gather x1, waiting for transfers between devices, per_device(): lax.all_gather(embeds, 'feat', axis=1, tiled=True)  43.2 us
    all_gather x1, blocking collectives, per_device(): full_weights = lax.all_gather(weights, 'clip', axis=1, tiled=True)  29.4 us
    dot_general x1, matrix products, per_device(): jnp.dot(lax.all_gather(embeds, 'feat', axis=1, tiled=True), freq_full, pr...  23.3 us
  transfers between devices with their start and end apart: 7, of which 7 were waited for; matrix products, arithmetic and copies ran while one was open for 1% of the time, Pallas kernels for 0%

commit v1 on v0

--- a/solution.py
+++ b/solution.py
@@ -8,7 +8,7 @@
 
 
 def summed_logits(partial_value):
-    return lax.psum(partial_value, "feat")
+    return jnp.sum(lax.all_gather(partial_value, "feat"), axis=0)
 
 
 def per_device(embeds, frequencies, phases, weights, labels):

time: 1090 us -> 726 us (0.67)
  waiting for transfers between devices: 954 us -> 567 us
  other arithmetic: 2.98 us -> 22.7 us
    psum x3 -> x0, waiting for transfers between devices: 696 us -> none  [summed_logits(): return lax.psum(partial_value, 'feat')]
    all_gather x0 -> x3, waiting for transfers between devices: none -> 313 us  [summed_logits(): return jnp.sum(lax.all_gather(partial_value, 'feat'), axis=0)]
    reduce_sum x0 -> x3, other arithmetic: none -> 19.8 us  [summed_logits(): return jnp.sum(lax.all_gather(partial_value, 'feat'), axis=0)]
where the time goes in v1:
time: 726 us
  waiting for transfers between devices  567 us (78%)
  blocking collectives  85.1 us (12%)
  matrix products  29.6 us (4%)
  other arithmetic  22.7 us (3%)
  between operations  14.2 us (2%)
    all_gather x3, waiting for transfers between devices, summed_logits(): return jnp.sum(lax.all_gather(partial_value, 'feat'), axis=0)  313 us
    reduce_scatter x2, waiting for transfers between devices, per_device(): lax.psum_scatter(grad_part, 'clip', scatter_dimension=1, tiled=True)  148 us
    all_gather x1, waiting for transfers between devices, per_device(): freq_full = lax.all_gather(frequencies, 'clip', axis=0, tiled=True)  61.4 us
    all_gather x2, blocking collectives, per_device(): lax.all_gather(own_weights.astype(jnp.bfloat16), 'clip', axis=1, tiled=True)  55.7 us
    all_gather x1, waiting for transfers between devices, per_device(): lax.all_gather(embeds, 'feat', axis=1, tiled=True)  43.2 us
    all_gather x1, blocking collectives, per_device(): full_weights = lax.all_gather(weights, 'clip', axis=1, tiled=True)  29.4 us
    dot_general x1, matrix products, per_device(): jnp.dot(lax.all_gather(embeds, 'feat', axis=1, tiled=True), freq_full, pr...  23.3 us
    reduce_sum x3, other arithmetic, summed_logits(): return jnp.sum(lax.all_gather(partial_value, 'feat'), axis=0)  19.8 us
  transfers between devices with their start and end apart: 7, of which 7 were waited for; matrix products, arithmetic and copies ran while one was open for 1% of the time, Pallas kernels for 0%

profile of v1, /device:TPU:1, one launch (start us, length us, event | category | flops | bytes accessed | tf_op | source)
XLA Modules:
  0.0 725.8 jit_solution(2039076470590351429)
XLA Ops:
  8.7 0.8 convert
  9.5 29.4 %all_gather.35 = bf16[640,128]{0,1:T(8,128)(2,1)S(1)} all-gather(bf16[640,16]{0,1:T(8,128)(2,1)S(1)} %convert), channel_id=1, replica_groups=mesh['clip'=8,'feat'=32] {'clip'}, dimensions={1}, use_global_device_ids=true | all-gather | bytes 184320 | tf_op jit(solution)/shard_map/all_gather | solution.py:28
  38.8 43.2 %all-gather.18.cloned.1.call-done = f32[32,36,1024]{2,1,0:T(8,128)} async-done(((f32[1,36,1024]{2,1,0:T(8,128)}), f32[32,36,1024]{2,1,0:T(8,128)}) %all-gather.18.cloned.1.call-update) | async-done | bytes 4718608 | tf_op jit(solution)/shard_map/all_gather | solution.py:21
  82.0 5.2 reshape.9
  87.3 61.4 %all-gather.10.cloned.1.call-done = f32[1152,640]{1,0:T(8,128)} async-done(((f32[144,640]{1,0:T(8,128)}), f32[1152,640]{1,0:T(8,128)}) %all-gather.10.cloned.1.call-update) | async-done | bytes 2949136 | tf_op jit(solution)/shard_map/all_gather | solution.py:15
  148.6 23.3 %multiply_convert_fusion = bf16[1024,640]{1,0:T(8,128)(2,1)S(1)} fusion(f32[1152,1024]{1,0:T(8,128)} %reshape.9, f32[1152,640]{1,0:T(8,128)} %all-gather.10.cloned.1.call-done, f32[640]{0:T(1024)S(1)} %copy-done.3), kind=kOutput, calls=%fused_computation | convolution fusion | flops 9061662720 | bytes 8980992 | tf_op jit(solution)/shard_map/dot_general | solution.py:20
  172.0 1.3 fusion.12
  173.5 98.7 %all-gather.12.cloned.1.call-done = f32[32768,128]{1,0:T(8,128)} async-done(((f32[1024,128]{1,0:T(8,128)}), f32[32768,128]{1,0:T(8,128)}) %all-gather.12.cloned.1.call-update) | async-done | bytes 16777232 | tf_op jit(solution)/shard_map/all_gather | solution.py:11
  272.2 6.6 reduce_sum.27
  278.9 1.2 fusion
  280.1 74.0 %reduce-scatter.3.cloned.1.call-done = f32[640,16]{0,1:T(8,128)} async-done(((f32[640,128]{0,1:T(8,128)}), f32[640,16]{0,1:T(8,128)}) %reduce-scatter.3.cloned.1.call-update) | async-done | bytes 40976 | tf_op jit(solution)/shard_map/reduce_scatter | solution.py:40
  354.1 0.8 fusion.6
  354.9 27.9 %all_gather.38 = bf16[640,128]{0,1:T(8,128)(2,1)S(1)} all-gather(bf16[640,16]{0,1:T(8,128)(2,1)S(1)} %fusion.6), channel_id=1, replica_groups=mesh['clip'=8,'feat'=32] {'clip'}, dimensions={1}, use_global_device_ids=true | all-gather | bytes 184320 | tf_op jit(solution)/shard_map/all_gather | solution.py:42
  382.8 1.3 fusion.10
  384.2 107.3 %all-gather.14.cloned.1.call-done = f32[32768,128]{1,0:T(8,128)} async-done(((f32[1024,128]{1,0:T(8,128)}), f32[32768,128]{1,0:T(8,128)}) %all-gather.14.cloned.1.call-update) | async-done | bytes 16777232 | tf_op jit(solution)/shard_map/all_gather | solution.py:11
  491.5 6.6 reduce_sum.28
  498.1 1.2 fusion.1
  499.3 74.0 %reduce-scatter.5.cloned.1.call-done = f32[640,16]{0,1:T(8,128)} async-done(((f32[640,128]{0,1:T(8,128)}), f32[640,16]{0,1:T(8,128)}) %reduce-scatter.5.cloned.1.call-update) | async-done | bytes 40976 | tf_op jit(solution)/shard_map/reduce_scatter | solution.py:40
  573.3 1.4 fusion.9
  574.8 27.9 %all_gather.41 = bf16[640,128]{0,1:T(8,128)(2,1)S(1)} all-gather(bf16[640,16]{0,1:T(8,128)(2,1)S(1)} %get-tuple-element.4), channel_id=1, replica_groups=mesh['clip'=8,'feat'=32] {'clip'}, dimensions={1}, use_global_device_ids=true | all-gather | bytes 184320 | tf_op jit(solution)/shard_map/all_gather | solution.py:42
  602.6 1.3 fusion.11
  604.0 107.4 %all-gather.16.cloned.1.call-done = f32[32768,128]{1,0:T(8,128)} async-done(((f32[1024,128]{1,0:T(8,128)}), f32[32768,128]{1,0:T(8,128)}) %all-gather.16.cloned.1.call-update) | async-done | bytes 16777232 | tf_op jit(solution)/shard_map/all_gather | solution.py:11
  711.3 6.6 reduce_sum.29
  718.1 0.8 copy.7
  (23 shorter events, 2.1 us)
Async XLA Ops:
  7.2 74.9 %all-gather.18.cloned.1.call-start = ((), (), s32[]{:S(2)}) async-start(), calls=%async_computation.8 | async-start | bytes 5406720 | tf_op jit(solution)/shard_map/all_gather | solution.py:21
  7.9 140.7 %all-gather.10.cloned.1.call-start = ((), (), s32[]{:S(2)}) async-start(), calls=%async_computation.2 | async-start | bytes 3317760 | tf_op jit(solution)/shard_map/all_gather | solution.py:15
  8.6 263.6 %all-gather.12.cloned.1.call-start = ((), (), s32[]{:S(2)}) async-start(), calls=%async_computation.5 | async-start | bytes 17301504 | tf_op jit(solution)/shard_map/all_gather | solution.py:11
  38.8 109.8 %copy-start.3 = (f32[640]{0:T(1024)S(1)}, f32[640]{0:T(1024)}, u32[]{:S(2)}) copy-start(f32[640]{0:T(1024)} %param.7) | copy-start | bytes 7684
  173.3 180.8 %reduce-scatter.3.cloned.1.call-start = ((), (), s32[]{:S(2)}) async-start(), calls=%async_computation.3 | async-start | bytes 368640 | tf_op jit(solution)/shard_map/reduce_scatter | solution.py:40
  272.2 6.6 copy-start.2
  278.8 75.3 %copy-start = (f32[640,16]{0,1:T(8,128)S(1)}, f32[640,16]{0,1:T(8,128)}, u32[]{:S(2)}) copy-start(f32[640,16]{0,1:T(8,128)} %param.8) | copy-start | bytes 122884
  280.0 211.5 %all-gather.14.cloned.1.call-start = ((), (), s32[]{:S(2)}) async-start(), calls=%async_computation.6 | async-start | bytes 17301504 | tf_op jit(solution)/shard_map/all_gather | solution.py:11
  384.1 189.2 %reduce-scatter.5.cloned.1.call-start = ((), (), s32[]{:S(2)}) async-start(), calls=%async_computation.4 | async-start | bytes 368640 | tf_op jit(solution)/shard_map/reduce_scatter | solution.py:40
  498.1 75.3 %copy-start.1 = (f32[640,16]{0,1:T(8,128)S(1)}, f32[640,16]{0,1:T(8,128)}, u32[]{:S(2)}) copy-start(f32[640,16]{0,1:T(8,128)} %reduce-scatter.3.cloned.1.call-done) | copy-start | bytes 122884
  499.3 212.1 %all-gather.16.cloned.1.call-start = ((), (), s32[]{:S(2)}) async-start(), calls=%async_computation.7 | async-start | bytes 17301504 | tf_op jit(solution)/shard_map/all_gather | solution.py:11
Sparse Core Ops, SparseCore 0:
  9.8 72.1 all-gather.17
  84.6 63.9 all-gather.9
  173.4 98.7 all-gather.11
  280.2 73.9 reduce-scatter.2
  384.2 107.2 all-gather.13
  499.4 73.9 reduce-scatter.4
  604.1 107.2 all-gather.15
